TPU v7x, 256 devices: a whole 4x4x8 slice. The times are simulated.
256 devices in a mesh: roll: 4 (over z_lo, core), mach: 16 (over y, x), cross: 4 (over z_hi).
Axes of the slice: x: 4, y: 4, z: 8 (z_hi: 4, z_lo: 2; z = z_hi * 2 + z_lo), core: 2. Of those that a mesh axis runs over, the one named last changes fastest.
Arguments:
- density: bfloat16 [128, 4096, 2048], P('roll', 'mach', 'cross'), may hold values from 0 to 1
- roll_start: float32 [32, 128], P(None, 'roll'), may hold values from 0.05 to 1
- mach_factor: bfloat16 [32, 4096], P(None, 'mach'), may hold values from 0.0099487305 to 1
- cross_factor: bfloat16 [32, 2048], P(None, 'cross'), may hold values from 0.0099487305 to 1
Outputs:
- roll_factor: float32 [32, 128], P(None, 'roll')
- mode_two: float32 [32, 4096], P(None, ('mach', 'cross'))
All inputs are finite; a program needn't handle non-finite values.
Results may differ from a plain program's by a relative error of at most 0.0003.
Values sent between devices are 32-bit elements; how exact they have to be, the bound alone decides.
A program may use at most 64 MiB of HBM per device.

v0:
```python
import jax
import jax.numpy as jnp
from jax import lax
from jax.sharding import PartitionSpec as P


def hals_rows(roll_rows, mttkrp, gram):

    def column_step(column, rows):
        column = jnp.asarray(column).astype(jnp.int32)
        gram_row = lax.dynamic_slice_in_dim(gram, column, 1, 0)
        diag_entry = lax.dynamic_slice_in_dim(gram_row, column, 1, 1)
        current = lax.dynamic_slice_in_dim(rows, column, 1, 0)
        target = lax.dynamic_slice_in_dim(mttkrp, column, 1, 0)
        mixed = jnp.dot(gram_row, rows, precision=lax.Precision.HIGHEST)
        updated = jnp.maximum(current + (target - mixed) / diag_entry, 0.0)
        return lax.dynamic_update_slice_in_dim(rows, updated, column, 0)

    return lax.fori_loop(0, roll_rows.shape[0], column_step, roll_rows)


def local(density, roll_start, mach_factor, cross_factor):
    rolls_here, bins_here, cross_here = density.shape
    rank = cross_factor.shape[0]
    flat = density.reshape(rolls_here * bins_here, cross_here)
    partial_value = lax.dot_general(
        cross_factor, flat, (((1,), (1,)), ((), ())), preferred_element_type=jnp.float32
    )
    partial_value = partial_value.reshape(rank, rolls_here, bins_here)
    local_terms = jnp.einsum(
        "rij,rj->ri",
        partial_value,
        mach_factor.astype(jnp.float32),
        precision=lax.Precision.HIGHEST,
    )
    local_mach = jnp.dot(mach_factor, mach_factor.T, preferred_element_type=jnp.float32)
    local_cross = jnp.dot(cross_factor, cross_factor.T, preferred_element_type=jnp.float32)
    mttkrp = lax.psum(local_terms, ("mach", "cross"))
    gram_mach = lax.psum(local_mach, "mach")
    gram_cross = lax.psum(local_cross, "cross")
    gram = gram_mach * gram_cross
    roll_factor = hals_rows(roll_start, mttkrp, gram)
    term = jnp.einsum("rij,ri->rj", partial_value, roll_factor, precision=lax.Precision.HIGHEST)
    whole = lax.psum(term, ("roll", "cross"))
    span = whole.shape[1] // lax.axis_size("cross")
    total = lax.dynamic_slice_in_dim(whole, lax.axis_index("cross") * span, span, 1)
    all_rolls = rolls_here * lax.axis_size("roll")
    all_cross = cross_here * lax.axis_size("cross")
    scale = rank / (all_rolls * all_cross)
    mode_two = total * scale
    return (roll_factor, mode_two)


def solution(mesh):
    in_specs = (P("roll", "mach", "cross"), P(None, "roll"), P(None, "mach"), P(None, "cross"))
    out_specs = (P(None, "roll"), P(None, ("mach", "cross")))
    return jax.shard_map(local, mesh=mesh, in_specs=in_specs, out_specs=out_specs, check_vma=False)
```

profile of v0, /device:TPU:1, one launch (start us, length us, event | category | flops | bytes accessed | tf_op | source)
XLA Modules:
  0.0 584.9 jit_solution(14968535453906031717)
XLA Ops:
  1.4 5.9 %fusion.9 = f32[32,32,256]{2,0,1:T(8,128)S(1)} fusion(bf16[32,256,512]{2,1,0:T(8,128)(2,1)} %param.6, bf16[32,512]{1,0:T(8,128)(2,1)S(1)} %copy-done), kind=kOutput, calls=%fused_computation.12 | convolution fusion | flops 268435456 | bytes 9469952 | tf_op jit(solution)/shard_map/dot_general | solution.py:26
  7.3 1.2 fusion.7
  8.5 327.1 %psum.28 = f32[32,32]{1,0:T(8,128)S(1)} all-reduce(f32[32,32]{1,0:T(8,128)S(1)} %bitcast.34), channel_id=1, replica_groups=mesh['roll'=4,'mach'=16,'cross'=4] {'mach','cross'}, use_global_device_ids=true, to_apply=%region_2.0 | all-reduce | flops 1024 | bytes 8192 | tf_op jit(solution)/shard_map/psum | solution.py:38
  335.7 56.2 %psum.29 = f32[32,32]{1,0:T(8,128)S(1)} all-reduce(f32[32,32]{1,0:T(8,128)S(1)} %fusion.12), channel_id=1, replica_groups=mesh['roll'=4,'mach'=16,'cross'=4] {'mach'}, use_global_device_ids=true, to_apply=%region_0.0 | all-reduce | flops 1024 | bytes 8192 | tf_op jit(solution)/shard_map/psum | solution.py:39
  392.0 12.7 %psum.30 = f32[32,32]{1,0:T(8,128)S(1)} all-reduce(f32[32,32]{1,0:T(8,128)S(1)} %fusion.13), channel_id=1, replica_groups=mesh['roll'=4,'mach'=16,'cross'=4] {'cross'}, use_global_device_ids=true, to_apply=%region_1.0 | all-reduce | flops 1024 | bytes 8192 | tf_op jit(solution)/shard_map/psum | solution.py:40
  404.7 45.2 %while.16 = (s32[]{:T(128)}, f32[32,32]{1,0:T(8,128)S(1)}, f32[32,32]{1,0:T(8,128)S(1)}, f32[32,32]{1,0:T(8,128)S(1)}, s32[]{:T(128)}, /*index=5*/s32[]{:T(128)}, s32[]{:T(128)}) while((s32[]{:T(128)}, f32[32,32]{1,0:T(8,128)S(1)}, f32[32,32]{1,0:T(8,128)S(1)}, f32[32,32]{1,0:T(8,128)S(1)}, s32[]{:T(128)}, /*index=5*/s32[]{:T(128)}, ...), condition=%wide.region_4.0_spmd, body=%wide.region_3.0_spmd.sunk | while | flops 12419 | bytes 19449 | solution.py:19
  405.3 0.8 fusion.26
  406.7 0.8 fusion.26
  408.1 0.8 fusion.26
  409.6 0.8 fusion.26
  411.0 0.8 fusion.26
  412.4 0.8 fusion.26
  413.8 0.8 fusion.26
  415.2 0.8 fusion.26
  416.6 0.8 fusion.26
  418.0 0.8 fusion.26
  419.4 0.8 fusion.26
  420.8 0.8 fusion.26
  422.3 0.8 fusion.26
  423.7 0.8 fusion.26
  425.1 0.8 fusion.26
  426.5 0.8 fusion.26
  429.3 0.8 fusion.26
  430.7 0.8 fusion.26
  432.1 0.8 fusion.26
  433.6 0.8 fusion.26
  435.0 0.8 fusion.26
  436.4 0.8 fusion.26
  437.8 0.8 fusion.26
  439.2 0.8 fusion.26
  449.9 1.3 fusion.5
  451.2 133.1 %psum.31 = f32[32,256]{1,0:T(8,128)S(1)} all-reduce(f32[32,256]{1,0:T(8,128)S(1)} %bitcast.33), channel_id=1, replica_groups=mesh['roll'=4,'mach'=16,'cross'=4] {'roll','cross'}, use_global_device_ids=true, to_apply=%region_5.0 | all-reduce | flops 8192 | bytes 65536 | tf_op jit(solution)/shard_map/psum | solution.py:44
  (85 shorter events, 27.6 us)
Async XLA Ops:
  0.6 0.8 copy-start
  0.6 404.1 %copy-start.2 = (f32[32,32]{1,0:T(8,128)S(1)}, f32[32,32]{1,0:T(8,128)}, u32[]{:S(2)}) copy-start(f32[32,32]{1,0:T(8,128)} %param.7) | copy-start | bytes 12292
  0.7 6.6 %copy-start.3 = (bf16[32,256]{1,0:T(8,128)(2,1)S(1)}, bf16[32,256]{1,0:T(8,128)(2,1)}, u32[]{:S(2)}) copy-start(bf16[32,256]{1,0:T(8,128)(2,1)} %param.8) | copy-start | bytes 49156
  449.9 135.0 %copy-start.1 = (f32[32,32]{1,0:T(8,128)}, f32[32,32]{1,0:T(8,128)S(1)}, u32[]{:S(2)}) copy-start(f32[32,32]{1,0:T(8,128)S(1)} %get-tuple-element.124) | copy-start | bytes 12292
where the time goes:
time: 585 us
  blocking collectives  529 us (90%)
  matrix products  33.6 us (6%)
  local copies, waits for them, and re-layouts  20.4 us (3%)
    psum x1, blocking collectives, local(): mttkrp = lax.psum(local_terms, ('mach', 'cross'))  327 us
    psum x1, blocking collectives, local(): whole = lax.psum(term, ('roll', 'cross'))  133 us
    psum x1, blocking collectives, local(): gram_mach = lax.psum(local_mach, 'mach')  56.2 us
    dot_general x32, matrix products, column_step(): mixed = jnp.dot(gram_row, rows, precision=lax.Precision.HIGHEST)  25 us
    dynamic_slice x32, local copies, waits for them, and re-layouts, column_step(): diag_entry = lax.dynamic_slice_in_dim(gram_row, column, 1, 1)  18.8 us
    psum x1, blocking collectives, local(): gram_cross = lax.psum(local_cross, 'cross')  12.7 us

commit v1 on v0

--- a/solution.py
+++ b/solution.py
@@ -36,7 +36,11 @@
     local_mach = jnp.dot(mach_factor, mach_factor.T, preferred_element_type=jnp.float32)
     local_cross = jnp.dot(cross_factor, cross_factor.T, preferred_element_type=jnp.float32)
     mttkrp = lax.psum(local_terms, ("mach", "cross"))
-    gram_mach = lax.psum(local_mach, "mach")
+    gram_mach = local_mach
+    for hop in (1, 2, 4, 8):
+        gram_mach = gram_mach + lax.ppermute(
+            gram_mach, "mach", [(dev, dev ^ hop) for dev in range(16)]
+        )
     gram_cross = lax.psum(local_cross, "cross")
     gram = gram_mach * gram_cross
     roll_factor = hals_rows(roll_start, mttkrp, gram)

time: 585 us -> 521 us (0.89)
  blocking collectives: 529 us -> 454 us
  starting transfers between devices: 0 us -> 8.58 us
    psum x1 -> x0, blocking collectives: 56.2 us -> none  [local(): gram_mach = lax.psum(local_mach, 'mach')]
    psum x1, blocking collectives: 133 us -> 119 us  [local(): whole = lax.psum(term, ('roll', 'cross'))]
    psum x1, blocking collectives: 327 us -> 317 us  [local(): mttkrp = lax.psum(local_terms, ('mach', 'cross'))]
    ppermute x0 -> x4, starting transfers between devices: none -> 8.58 us  [local(): lax.ppermute(gram_mach, 'mach', [(dev, dev ^ hop) for dev in range(16)])]
  transfers between devices with their start and end apart: 0 -> 4, of which waited for: 0 -> 1; matrix products, arithmetic and copies ran while one was open for 0% -> 1% of each run, Pallas kernels for 0% -> 0%
where the time goes in v1:
time: 521 us
  blocking collectives  454 us (87%)
  matrix products  34.4 us (7%)
  local copies, waits for them, and re-layouts  19.7 us (4%)
  starting transfers between devices  8.58 us (2%)
    psum x1, blocking collectives, local(): mttkrp = lax.psum(local_terms, ('mach', 'cross'))  317 us
    psum x1, blocking collectives, local(): whole = lax.psum(term, ('roll', 'cross'))  119 us
    dot_general x32, matrix products, column_step(): mixed = jnp.dot(gram_row, rows, precision=lax.Precision.HIGHEST)  25 us
    dynamic_slice x32, local copies, waits for them, and re-layouts, column_step(): diag_entry = lax.dynamic_slice_in_dim(gram_row, column, 1, 1)  18.8 us
    psum x1, blocking collectives, local(): gram_cross = lax.psum(local_cross, 'cross')  18.5 us
  transfers between devices with their start and end apart: 4, of which 1 were waited for; matrix products, arithmetic and copies ran while one was open for 1% of the time, Pallas kernels for 0%

profile of v1, /device:TPU:1, one launch (start us, length us, event | category | flops | bytes accessed | tf_op | source)
XLA Modules:
  0.0 520.6 jit_solution(14580374367611063691)
XLA Ops:
  0.7 0.9 fusion.12
  1.6 2.0 collective-permute-start
  3.6 5.9 %fusion.9 = f32[32,32,256]{2,0,1:T(8,128)S(1)} fusion(bf16[32,256,512]{2,1,0:T(8,128)(2,1)} %param.6, bf16[32,512]{1,0:T(8,128)(2,1)S(1)} %copy-done), kind=kOutput, calls=%fused_computation.12 | convolution fusion | flops 268435456 | bytes 9469952 | tf_op jit(solution)/shard_map/dot_general | solution.py:26
  9.6 1.2 fusion.7
  10.8 2.5 collective-permute-start.1
  13.4 1.5 collective-permute-done.1
  14.9 1.3 collective-permute-start.2
  16.2 18.5 %psum.22 = f32[32,32]{1,0:T(8,128)S(1)} all-reduce(f32[32,32]{1,0:T(8,128)S(1)} %fusion.13), channel_id=1, replica_groups=mesh['roll'=4,'mach'=16,'cross'=4] {'cross'}, use_global_device_ids=true, to_apply=%region_0.0 | all-reduce | flops 1024 | bytes 8192 | tf_op jit(solution)/shard_map/psum | solution.py:44
  34.7 2.7 collective-permute-start.3
  37.4 316.6 %psum.21 = f32[32,32]{1,0:T(8,128)S(1)} all-reduce(f32[32,32]{1,0:T(8,128)S(1)} %bitcast.34), channel_id=1, replica_groups=mesh['roll'=4,'mach'=16,'cross'=4] {'mach','cross'}, use_global_device_ids=true, to_apply=%region_1.0 | all-reduce | flops 1024 | bytes 8192 | tf_op jit(solution)/shard_map/psum | solution.py:38
  354.0 45.2 %while.16 = (s32[]{:T(128)}, f32[32,32]{1,0:T(8,128)S(1)}, f32[32,32]{1,0:T(8,128)S(1)}, f32[32,32]{1,0:T(8,128)S(1)}, s32[]{:T(128)}, /*index=5*/s32[]{:T(128)}, s32[]{:T(128)}) while((s32[]{:T(128)}, f32[32,32]{1,0:T(8,128)S(1)}, f32[32,32]{1,0:T(8,128)S(1)}, f32[32,32]{1,0:T(8,128)S(1)}, s32[]{:T(128)}, /*index=5*/s32[]{:T(128)}, ...), condition=%wide.region_3.0_spmd, body=%wide.region_2.0_spmd.sunk | while | flops 12419 | bytes 19949 | solution.py:19
  354.6 0.8 fusion.26
  356.0 0.8 fusion.26
  357.5 0.8 fusion.26
  358.9 0.8 fusion.26
  360.3 0.8 fusion.26
  361.7 0.8 fusion.26
  363.1 0.8 fusion.26
  364.5 0.8 fusion.26
  365.9 0.8 fusion.26
  367.3 0.8 fusion.26
  368.7 0.8 fusion.26
  371.6 0.8 fusion.26
  373.0 0.8 fusion.26
  374.4 0.8 fusion.26
  375.8 0.8 fusion.26
  377.2 0.8 fusion.26
  378.6 0.8 fusion.26
  380.0 0.8 fusion.26
  381.4 0.8 fusion.26
  399.2 1.3 fusion.5
  400.5 119.4 %psum.23 = f32[32,256]{1,0:T(8,128)S(1)} all-reduce(f32[32,256]{1,0:T(8,128)S(1)} %bitcast.33), channel_id=1, replica_groups=mesh['roll'=4,'mach'=16,'cross'=4] {'roll','cross'}, use_global_device_ids=true, to_apply=%region_4.0 | all-reduce | flops 8192 | bytes 65536 | tf_op jit(solution)/shard_map/psum | solution.py:48
  (95 shorter events, 30.7 us)
Async XLA Ops:
  0.6 3.0 copy-start
  0.6 8.9 %copy-start.3 = (bf16[32,256]{1,0:T(8,128)(2,1)S(1)}, bf16[32,256]{1,0:T(8,128)(2,1)}, u32[]{:S(2)}) copy-start(bf16[32,256]{1,0:T(8,128)(2,1)} %param.8) | copy-start | bytes 49156
  0.7 353.4 %copy-start.2 = (f32[32,32]{1,0:T(8,128)S(1)}, f32[32,32]{1,0:T(8,128)}, u32[]{:S(2)}) copy-start(f32[32,32]{1,0:T(8,128)} %param.7) | copy-start | bytes 12292
  1.6 9.2 %collective-permute-start = (f32[32,32]{1,0:T(8,128)S(1)}, f32[32,32]{1,0:T(8,128)S(1)}, u32[]{:S(2)}, u32[]{:S(2)}) collective-permute-start(f32[32,32]{1,0:T(8,128)S(1)} %fusion.12), channel_id=1, source_target_pairs={{0,4},{4,0},{8,12},{12,8},{16,20},{20,16},{24,28},{28,24},{32,36},... | collective-permute-start | bytes 12296 | tf_op jit(solution)/shard_map/ppermute | solution.py:41
  10.8 4.2 collective-permute-start.1
  14.9 19.8 %collective-permute-start.2 = (f32[32,32]{1,0:T(8,128)S(1)}, f32[32,32]{1,0:T(8,128)S(1)}, u32[]{:S(2)}, u32[]{:S(2)}) collective-permute-start(f32[32,32]{1,0:T(8,128)S(1)} %add.79), channel_id=1, source_target_pairs={{0,16},{4,20},{8,24},{12,28},{16,0},{20,4},{24,8},{28,12},{32,48},... | collective-permute-start | bytes 12296 | tf_op jit(solution)/shard_map/ppermute | solution.py:41
  34.7 319.3 %collective-permute-start.3 = (f32[32,32]{1,0:T(8,128)S(1)}, f32[32,32]{1,0:T(8,128)S(1)}, u32[]{:S(2)}, u32[]{:S(2)}) collective-permute-start(f32[32,32]{1,0:T(8,128)S(1)} %add.80), channel_id=1, source_target_pairs={{0,32},{4,36},{8,40},{12,44},{16,48},{20,52},{24,56},{28,60},{32,0... | collective-permute-start | bytes 12296 | tf_op jit(solution)/shard_map/ppermute | solution.py:41
  399.2 121.4 %copy-start.1 = (f32[32,32]{1,0:T(8,128)}, f32[32,32]{1,0:T(8,128)S(1)}, u32[]{:S(2)}) copy-start(f32[32,32]{1,0:T(8,128)S(1)} %get-tuple-element.124) | copy-start | bytes 12292
